TPU v7x, 512 devices: a whole 4x8x8 slice. The times are simulated.
512 devices in a mesh: bead: 32 (over y_lo, z, core), slab: 16 (over y_hi, x).
Axes of the slice: x: 4, y: 8 (y_hi: 4, y_lo: 2; y = y_hi * 2 + y_lo), z: 8, core: 2. Of those that a mesh axis runs over, the one named last changes fastest.
Arguments:
- positions: float32 [32, 3, 16, 4, 4, 128], P('bead', None, 'slab'), may hold values from 0 to 1
- velocities: float32 [32, 3, 16, 4, 4, 128], P('bead', None, 'slab'), may hold values from -6 to 6
- counts: int32 [16, 4, 4], P('slab'), may hold values from 64 to 128
Outputs:
- positions_out: float32 [32, 3, 16, 4, 4, 128], P('bead', None, 'slab')
- velocities_out: float32 [32, 3, 16, 4, 4, 128], P('bead', None, 'slab')
Inputs may be any that keep to these rules, and one draw needn't show every extreme that they name: `counts`: a cell's atoms occupy its slots 0 to count - 1; the other slots are empty.
All inputs are finite; a program needn't handle non-finite values.
Results may differ from a plain program's by a relative error of at most 0.0001.
Values sent between devices are 32-bit elements; how exact they have to be, the bound alone decides.
A program may use at most 64 MiB of HBM per device.

v0:
```python
import functools

import jax
import jax.numpy as jnp
from jax import lax
from jax.experimental import pallas as pl
from jax.experimental.pallas import tpu as pltpu
from jax.sharding import PartitionSpec as P

STEPS = 4
EVALS = STEPS + 1

PAIR_SCALE = 0.08
WIDTH_FACTOR = 2.0
SPRING = 4.0
HALF_STEP = 0.025
TIME_STEP = 0.05

LOG2E = 1.4426950408889634
ALPHA = WIDTH_FACTOR * LOG2E
ABSENT = -1e30

CELLS = 16
SLOTS = 128
FEATS = 32
MESH = pl.DeviceIdType.MESH


def split3(value):
    high = value.astype(jnp.bfloat16).astype(jnp.float32)
    rest = value - high
    mid = rest.astype(jnp.bfloat16).astype(jnp.float32)
    return high, mid, rest - mid


def far_rows(coords):
    rows = []
    for coord in coords:
        h, m, l = split3(coord)
        rows += [h, m, l, h, m, h]
    norm = -ALPHA * (coords[0] * coords[0] + coords[1] * coords[1] + coords[2] * coords[2])
    return rows + list(split3(norm))


def own_rows(coords):
    rows = []
    for coord in coords:
        h, m, l = split3((2.0 * ALPHA) * coord)
        rows += [h, h, h, m, m, l]
    norm = -ALPHA * (coords[0] * coords[0] + coords[1] * coords[1] + coords[2] * coords[2])
    return rows, list(split3(norm))


def kernel(
    beads, slabs,
    pos_in, vel_in, counts, pos_out, vel_out,
    qs, halo, chain, mask_own, mask_halo, ext, own32, far32, own_feats, far_feats,
    bcast, acc, sums, eye, pick,
    send_sem, recv_sem, mask_send, mask_recv, load_sem,
):
    bead, slab = lax.axis_index("bead"), lax.axis_index("slab")
    slab_up, slab_down = lax.rem(slab + 1, slabs), lax.rem(slab + slabs - 1, slabs)
    bead_up, bead_down = lax.rem(bead + 1, beads), lax.rem(bead + beads - 1, beads)
    partners = [(bead, slab_up), (bead, slab_down), (bead_up, slab), (bead_down, slab)]

    barrier = pltpu.get_barrier_semaphore()
    for partner in partners:
        pl.semaphore_signal(barrier, inc=1, device_id=partner, device_id_type=MESH)

    lanes = lax.broadcasted_iota(jnp.int32, (1, SLOTS), 1)
    for cell in range(CELLS):
        here = lanes < counts[0, cell // 4, cell % 4]
        mask_own[cell : cell + 1, :] = jnp.where(here, 0.0, ABSENT)
    qs[0] = pos_in[...]
    vel_out[...] = vel_in[...]

    one = jnp.ones((8, SLOTS), jnp.float32)
    zero = jnp.zeros((8, SLOTS), jnp.float32)
    for group in range(6):
        for row in (18, 19, 20, 24):
            own32[pl.ds(group * 8 * FEATS + row, 8, stride=FEATS), :] = one
        for row in range(25, FEATS):
            own32[pl.ds(group * 8 * FEATS + row, 8, stride=FEATS), :] = zero
    for group in range(6):
        for row in (21, 22, 23):
            far32[pl.ds(group * 8 * FEATS + row, 8, stride=FEATS), :] = one
        for row in range(25, FEATS):
            far32[pl.ds(group * 8 * FEATS + row, 8, stride=FEATS), :] = zero
    ext[...] = jnp.zeros_like(ext)
    row_id = lax.broadcasted_iota(jnp.int32, (SLOTS, SLOTS), 0)
    lane_id = lax.broadcasted_iota(jnp.int32, (SLOTS, SLOTS), 1)
    eye[...] = jnp.where(row_id == lane_id, 1.0, 0.0).astype(jnp.bfloat16)
    feat_id = lax.broadcasted_iota(jnp.int32, (FEATS, SLOTS), 0)
    for comp in range(3):
        first = 6 * comp
        chosen = (feat_id >= first) & (feat_id < first + 3)
        pick[:, comp * SLOTS : (comp + 1) * SLOTS] = jnp.where(chosen, 1.0, 0.0).astype(jnp.bfloat16)

    pl.semaphore_wait(barrier, 4)

    def mask_copy(side):
        return pltpu.make_async_remote_copy(
            src_ref=mask_own,
            dst_ref=mask_halo.at[1 - side],
            send_sem=mask_send.at[side],
            recv_sem=mask_recv.at[1 - side],
            device_id=partners[side],
            device_id_type=MESH,
        )

    def slab_copy(turn, side):
        return pltpu.make_async_remote_copy(
            src_ref=qs.at[turn],
            dst_ref=halo.at[turn, 1 - side],
            send_sem=send_sem.at[turn, side],
            recv_sem=recv_sem.at[turn, 1 - side],
            device_id=partners[side],
            device_id_type=MESH,
        )

    def bead_copy(turn, side):
        return pltpu.make_async_remote_copy(
            src_ref=qs.at[turn],
            dst_ref=chain.at[turn, 1 - side],
            send_sem=send_sem.at[turn, 2 + side],
            recv_sem=recv_sem.at[turn, 3 - side],
            device_id=partners[2 + side],
            device_id_type=MESH,
        )

    for side in range(2):
        mask_copy(side).start()

    cell_id = lax.broadcasted_iota(jnp.int32, (CELLS, SLOTS), 0)
    off_y = (cell_id // 4).astype(jnp.float32) - 2.0
    off_z = (cell_id % 4).astype(jnp.float32) - 2.0

    def put_far(layer, coords, masks):
        for half in range(2):
            sel = slice(8 * half, 8 * half + 8)
            rows = far_rows([coord[sel] for coord in coords])
            base = (layer * CELLS + 8 * half) * FEATS
            for k, row in enumerate(rows):
                far32[pl.ds(base + k, 8, stride=FEATS), :] = row
            far32[pl.ds(base + 24, 8, stride=FEATS), :] = masks[sel]
        for cell in range(CELLS):
            at = layer * CELLS + cell
            block = far32[at * FEATS : (at + 1) * FEATS, :].astype(jnp.bfloat16)
            turned = lax.dot_general(
                eye[...], block, (((1,), (1,)), ((), ())), preferred_element_type=jnp.float32
            )
            far_feats[at] = turned.astype(jnp.bfloat16)

    def put_own(q):
        for comp in range(3):
            for yy in range(6):
                y = (yy + 3) % 4
                first = comp * CELLS + 4 * y
                ext[comp, yy, 1:5, :] = q[first : first + 4]
                ext[comp, yy, 0:1, :] = q[first + 3 : first + 4]
                ext[comp, yy, 5:6, :] = q[first : first + 1]
        zz_off = lax.broadcasted_iota(jnp.int32, (8, SLOTS), 0).astype(jnp.float32) - 3.0
        for yy in range(6):
            coords = [ext[0, yy] - 0.5, ext[1, yy] + (yy - 3.0), ext[2, yy] + zz_off]
            rows, norm = own_rows(coords)
            base = yy * 8 * FEATS
            for k, row in enumerate(rows):
                own32[pl.ds(base + k, 8, stride=FEATS), :] = row
            for k, row in enumerate(norm):
                own32[pl.ds(base + 21 + k, 8, stride=FEATS), :] = row
        for yy in range(6):
            for zz in range(6):
                at = (yy * 8 + zz) * FEATS
                own_feats[yy, :, zz * SLOTS : (zz + 1) * SLOTS] = own32[at : at + FEATS, :].astype(
                    jnp.bfloat16
                )

    def pairs(group):
        ny = lax.rem(group, 4)
        for nz in range(4):
            feats = far_feats[group * 4 + nz]
            bcast[nz] = jnp.dot(feats, pick[...], preferred_element_type=jnp.float32)
            for dy in range(3):
                yy = ny + dy
                expo = jnp.dot(
                    feats,
                    own_feats[yy, :, nz * SLOTS : (nz + 3) * SLOTS],
                    preferred_element_type=jnp.float32,
                )
                parts = [[None] * 4 for _ in range(3)]
                for chunk in range(SLOTS // 8):
                    sel = slice(8 * chunk, 8 * chunk + 8)
                    far = [bcast[nz, sel, k * SLOTS : (k + 1) * SLOTS] for k in range(3)]
                    for dz in range(3):
                        w = jnp.exp2(expo[sel, dz * SLOTS : (dz + 1) * SLOTS])
                        terms = [w, w * far[0], w * far[1], w * far[2]]
                        for k in range(4):
                            old = parts[dz][k]
                            parts[dz][k] = terms[k] if old is None else old + terms[k]
                for dz in range(3):
                    for k in range(4):
                        acc[yy, nz + dz, k] += parts[dz][k]

    def turn_body(turn, carry):
        for side in range(2):
            slab_copy(turn, side).start()
            bead_copy(turn, side).start()
        q = qs[turn]
        x, y, z = q[0:16] - 0.5, q[16:32] + off_y, q[32:48] + off_z
        acc[...] = jnp.zeros_like(acc)
        put_own(q)
        put_far(0, [x, y, z], mask_own[...])

        @pl.loop(0, 4)
        def _(group):
            pairs(group)

        @pl.when(turn == 0)
        def _():
            for side in range(2):
                mask_copy(side).wait()

        for side in range(2):
            slab_copy(turn, side).wait()
        for side in range(2):
            near = halo[turn, side]
            shift = 0.5 if side == 0 else -1.5
            put_far(
                1 + side,
                [near[0:16] + shift, near[16:32] + off_y, near[32:48] + off_z],
                mask_halo[side],
            )

        @pl.loop(4, 12)
        def _(group):
            pairs(group)

        for cell in range(CELLS):
            cy, cz = cell // 4, cell % 4
            ys = [(cy + 1, 0.0)] + ([(5, 4.0)] if cy == 0 else []) + ([(0, -4.0)] if cy == 3 else [])
            zs = [(cz + 1, 0.0)] + ([(5, 4.0)] if cz == 0 else []) + ([(0, -4.0)] if cz == 3 else [])
            total = [None] * 4
            for yy, sy in ys:
                for zz, sz in zs:
                    got = [acc[yy, zz, k] for k in range(4)]
                    if sy:
                        got[2] = got[2] - sy * got[0]
                    if sz:
                        got[3] = got[3] - sz * got[0]
                    total = [g if t is None else t + g for t, g in zip(total, got)]
            for k in range(4):
                sums[k, cell : cell + 1, :] = jnp.sum(total[k], axis=0, keepdims=True)

        for side in range(2):
            bead_copy(turn, side).wait()
        before, behind = chain[turn, 1], chain[turn, 0]
        spring = -SPRING * ((2.0 * q - before) - behind)
        here = jnp.where(mask_own[...] == 0.0, PAIR_SCALE, 0.0)
        force = [
            (coord * sums[0] - sums[1 + k]) * here + spring[16 * k : 16 * k + 16]
            for k, coord in enumerate([x, y, z])
        ]
        finish = jnp.where(turn > 0, HALF_STEP, 0.0)
        begin = jnp.where(turn < STEPS, HALF_STEP, 0.0)
        after = jnp.minimum(turn + 1, STEPS)
        for k in range(3):
            sel = slice(16 * k, 16 * k + 16)
            v = vel_out[sel] + finish * force[k]
            v = v + begin * force[k]
            vel_out[sel] = v

            @pl.when(turn < STEPS)
            def _():
                qs[after, sel] = q[sel] + TIME_STEP * v
        return carry

    lax.fori_loop(0, EVALS, turn_body, 0)
    pos_out[...] = qs[STEPS]


def local(positions, velocities, counts):
    rows = 3 * CELLS
    beads, slabs = lax.axis_size("bead"), lax.axis_size("slab")
    f32, bf16 = jnp.float32, jnp.bfloat16
    vmem = pl.BlockSpec(memory_space=pltpu.VMEM)
    out = pl.pallas_call(
        functools.partial(kernel, beads, slabs),
        out_shape=[jax.ShapeDtypeStruct((rows, SLOTS), f32)] * 2,
        in_specs=[vmem, vmem, pl.BlockSpec(memory_space=pltpu.SMEM)],
        out_specs=[vmem, vmem],
        scratch_shapes=[
            pltpu.VMEM((EVALS, rows, SLOTS), f32),
            pltpu.VMEM((EVALS, 2, rows, SLOTS), f32),
            pltpu.VMEM((EVALS, 2, rows, SLOTS), f32),
            pltpu.VMEM((CELLS, SLOTS), f32),
            pltpu.VMEM((2, CELLS, SLOTS), f32),
            pltpu.VMEM((3, 6, 8, SLOTS), f32),
            pltpu.VMEM((48 * FEATS, SLOTS), f32),
            pltpu.VMEM((48 * FEATS, SLOTS), f32),
            pltpu.VMEM((6, FEATS, 6 * SLOTS), bf16),
            pltpu.VMEM((48, SLOTS, FEATS), bf16),
            pltpu.VMEM((4, SLOTS, 3 * SLOTS), f32),
            pltpu.VMEM((6, 6, 4, 8, SLOTS), f32),
            pltpu.VMEM((4, CELLS, SLOTS), f32),
            pltpu.VMEM((SLOTS, SLOTS), bf16),
            pltpu.VMEM((FEATS, 3 * SLOTS), bf16),
            pltpu.SemaphoreType.DMA((EVALS, 4)),
            pltpu.SemaphoreType.DMA((EVALS, 4)),
            pltpu.SemaphoreType.DMA((2,)),
            pltpu.SemaphoreType.DMA((2,)),
            pltpu.SemaphoreType.DMA((2,)),
        ],
        compiler_params=pltpu.CompilerParams(collective_id=0, has_side_effects=True),
        name="verlet",
    )(positions.reshape(rows, SLOTS), velocities.reshape(rows, SLOTS), counts)
    return tuple(o.reshape(positions.shape) for o in out)


def solution(mesh):
    spec = P("bead", None, "slab", None, None, None)
    return jax.shard_map(
        local,
        mesh=mesh,
        in_specs=(spec, spec, P("slab", None, None)),
        out_specs=(spec, spec),
        check_vma=False,
    )
```

profile of v0, /device:TPU:8, one launch (start us, length us, event | category | flops | bytes accessed | tf_op | source)
XLA Modules:
  0.0 85.5 jit_solution(18113003251394900648)
XLA Ops:
  0.6 82.8 %verlet.1 = (f32[48,128]{1,0:T(8,128)}, f32[48,128]{1,0:T(8,128)}) custom-call(f32[48,128]{1,0:T(8,128)} %bitcast.8, f32[48,128]{1,0:T(8,128)} %bitcast.9, s32[1,4,4]{2,1,0:T(4,128)} %counts.1), custom_call_target="tpu_custom_call" | custom-call | tf_op jit(solution)/shard_map/verlet/pallas_call | solution.py:286
  83.5 0.0 copy-start
  83.5 1.4 %copy.9 = f32[1,3,1,4,4,128]{5,4,3,2,1,0:T(4,128)} copy(f32[1,3,1,4,4,128]{5,4,3,2,1,0:T(4,128)} %bitcast.11) | data formatting | bytes 49152
  84.8 0.0 copy-done
  84.8 0.6 copy.10
Async XLA Ops:
  83.5 1.4 %copy-start = (f32[48,128]{1,0:T(8,128)S(1)}, f32[48,128]{1,0:T(8,128)}, u32[]{:S(2)}) copy-start(f32[48,128]{1,0:T(8,128)} %get-tuple-element.5) | copy-start | bytes 73732
where the time goes:
time: 85.7 us; the launch traced here: 85.5 us
  Pallas kernels  82.8 us (97%)
  local copies, waits for them, and re-layouts  1.96 us (2%)
    pallas_call x1, Pallas kernels, local(): pl.pallas_call(functools.partial(kernel, beads, slabs), out_shape=[jax.Sh...  82.8 us
    unnamed x4, local copies, waits for them, and re-layouts  1.96 us

commit v1 on v0

v1 whole, which is shorter than its diff:
```python
import functools

import jax
import jax.numpy as jnp
from jax import lax
from jax.experimental import pallas as pl
from jax.experimental.pallas import tpu as pltpu
from jax.sharding import PartitionSpec as P

STEPS = 4
EVALS = STEPS + 1

PAIR_SCALE = 0.08
WIDTH_FACTOR = 2.0
SPRING = 4.0
HALF_STEP = 0.025
TIME_STEP = 0.05

LOG2E = 1.4426950408889634
ALPHA = WIDTH_FACTOR * LOG2E
ABSENT = -1e30

CELLS = 16
SLOTS = 128
FEATS = 32
OWN_STRIDE, FAR_STRIDE = 33, 25
UNROLL = 16
MESH = pl.DeviceIdType.MESH


def split3(value):
    high = value.astype(jnp.bfloat16).astype(jnp.float32)
    rest = value - high
    mid = rest.astype(jnp.bfloat16).astype(jnp.float32)
    return high, mid, rest - mid


def far_rows(coords):
    rows = []
    for coord in coords:
        h, m, l = split3(coord)
        rows += [h, m, l, h, m, h]
    norm = -ALPHA * (coords[0] * coords[0] + coords[1] * coords[1] + coords[2] * coords[2])
    return rows + list(split3(norm))


def own_rows(coords):
    rows = []
    for coord in coords:
        h, m, l = split3((2.0 * ALPHA) * coord)
        rows += [h, h, h, m, m, l]
    norm = -ALPHA * (coords[0] * coords[0] + coords[1] * coords[1] + coords[2] * coords[2])
    return list(enumerate(rows)) + list(enumerate(split3(norm), 21))


def kernel(
    beads, slabs,
    pos_in, vel_in, counts, pos_out, vel_out,
    qs, halo, chain, mask_own, mask_halo, ext, own32, far32, own_feats, far_feats, far_coords,
    acc, columns, sums, eye,
    send_sem, recv_sem, mask_send, mask_recv,
):
    bead, slab = lax.axis_index("bead"), lax.axis_index("slab")
    slab_up, slab_down = lax.rem(slab + 1, slabs), lax.rem(slab + slabs - 1, slabs)
    bead_up, bead_down = lax.rem(bead + 1, beads), lax.rem(bead + beads - 1, beads)
    partners = [(bead, slab_up), (bead, slab_down), (bead_up, slab), (bead_down, slab)]
    near = jnp.where(lax.rem(slab, 4) == 3, 1, 0)
    order = [near, 1 - near]

    barrier = pltpu.get_barrier_semaphore()
    for partner in partners:
        pl.semaphore_signal(barrier, inc=1, device_id=partner, device_id_type=MESH)

    lanes = lax.broadcasted_iota(jnp.int32, (1, SLOTS), 1)
    for cell in range(CELLS):
        here = lanes < counts[0, cell // 4, cell % 4]
        mask_own[cell : cell + 1, :] = jnp.where(here, 0.0, ABSENT)
    qs[0] = pos_in[...]
    vel_out[...] = vel_in[...]

    pl.semaphore_wait(barrier, 4)

    def mask_copy(side):
        return pltpu.make_async_remote_copy(
            src_ref=mask_own,
            dst_ref=mask_halo.at[1 - side],
            send_sem=mask_send.at[side],
            recv_sem=mask_recv.at[1 - side],
            device_id=partners[side],
            device_id_type=MESH,
        )

    def slab_copy(turn, side):
        return pltpu.make_async_remote_copy(
            src_ref=qs.at[turn],
            dst_ref=halo.at[turn, 1 - side],
            send_sem=send_sem.at[turn, side],
            recv_sem=recv_sem.at[turn, 1 - side],
            device_id=partners[side],
            device_id_type=MESH,
        )

    def slab_landing(turn, side):
        return pltpu.make_async_remote_copy(
            src_ref=qs.at[turn],
            dst_ref=halo.at[turn, side],
            send_sem=send_sem.at[turn, 0],
            recv_sem=recv_sem.at[turn, side],
            device_id=partners[0],
            device_id_type=MESH,
        )

    def bead_copy(turn, side):
        return pltpu.make_async_remote_copy(
            src_ref=qs.at[turn],
            dst_ref=chain.at[turn, 1 - side],
            send_sem=send_sem.at[turn, 2 + side],
            recv_sem=recv_sem.at[turn, 3 - side],
            device_id=partners[2 + side],
            device_id_type=MESH,
        )

    def send(turn):
        for side in range(2):
            slab_copy(turn, side).start()
        for side in range(2):
            bead_copy(turn, side).start()

    for side in range(2):
        mask_copy(side).start()
    send(0)

    one = jnp.ones((8, SLOTS), jnp.float32)
    zero = jnp.zeros((8, SLOTS), jnp.float32)
    for group in range(2):
        for row in range(FEATS):
            if row in (18, 19, 20) or row >= 24:
                at = pl.ds(group * 8 * OWN_STRIDE + row, 8, stride=OWN_STRIDE)
                own32[at, :] = one if row <= 24 else zero
    for group in range(18):
        for row in (21, 22, 23):
            far32[pl.ds(group * 8 * FAR_STRIDE + row, 8, stride=FAR_STRIDE), :] = one
    far32[3 * 48 * FAR_STRIDE :, :] = zero
    ext[...] = jnp.zeros_like(ext)
    columns[...] = jnp.zeros_like(columns)
    row_id = lax.broadcasted_iota(jnp.int32, (SLOTS, SLOTS), 0)
    lane_id = lax.broadcasted_iota(jnp.int32, (SLOTS, SLOTS), 1)
    eye[...] = jnp.where(row_id == lane_id, 1.0, 0.0).astype(jnp.bfloat16)

    cell_id = lax.broadcasted_iota(jnp.int32, (CELLS, SLOTS), 0)
    off_y = (cell_id // 4).astype(jnp.float32) - 2.0
    off_z = (cell_id % 4).astype(jnp.float32) - 2.0
    zz_off = lax.broadcasted_iota(jnp.int32, (8, SLOTS), 0).astype(jnp.float32) - 3.0
    lane8 = lax.broadcasted_iota(jnp.int32, (8, SLOTS), 1)

    def extend(comp, rows):
        for yy in range(6):
            y = (yy + 3) % 4
            ext[comp, yy, 1:5, :] = rows[4 * y : 4 * y + 4]
            ext[comp, yy, 0:1, :] = rows[4 * y + 3 : 4 * y + 4]
            ext[comp, yy, 5:6, :] = rows[4 * y : 4 * y + 1]

    def put_mask(slot, mask):
        extend(0, mask)
        for yy in range(6):
            far32[pl.ds((slot * 48 + yy * 8) * FAR_STRIDE + 24, 8, stride=FAR_STRIDE), :] = ext[0, yy]

    def put_far(slot, q, shift):
        for comp in range(3):
            extend(comp, q[16 * comp : 16 * comp + 16])
        for yy in range(6):
            coords = [ext[0, yy] + shift, ext[1, yy] + (yy - 3.0), ext[2, yy] + zz_off]
            for comp in range(3):
                far_coords[slot, comp, yy] = coords[comp]
            base = (slot * 48 + yy * 8) * FAR_STRIDE
            for k, row in enumerate(far_rows(coords)):
                far32[pl.ds(base + k, 8, stride=FAR_STRIDE), :] = row
        for yy in range(6):
            for zz in range(6):
                at = (slot * 48 + yy * 8 + zz) * FAR_STRIDE
                far_feats[slot, yy, :, zz * SLOTS : (zz + 1) * SLOTS] = far32[
                    at : at + FEATS, :
                ].astype(jnp.bfloat16)

    def put_own(coords):
        for half in range(2):
            sel = slice(8 * half, 8 * half + 8)
            for k, row in own_rows([coord[sel] for coord in coords]):
                own32[pl.ds(8 * half * OWN_STRIDE + k, 8, stride=OWN_STRIDE), :] = row
        for cell in range(CELLS):
            block = own32[cell * OWN_STRIDE : cell * OWN_STRIDE + FEATS, :].astype(jnp.bfloat16)
            turned = lax.dot_general(
                eye[...], block, (((1,), (1,)), ((), ())), preferred_element_type=jnp.float32
            )
            own_feats[cell] = turned.astype(jnp.bfloat16)

    def pairs(cell, blocks, first, last):
        cy, cz = cell // 4, lax.rem(cell, 4)
        feats = own_feats[cell]
        for start in range(0, len(blocks), 4):
            group = blocks[start : start + 4]
            opening, closing = first and start == 0, last and start + 4 >= len(blocks)
            expo, far = [], []
            for tile in range(0, len(group), 2):
                sides = [
                    far_feats[slot, cy + dy, :, pl.ds(pl.multiple_of((cz + dz) * SLOTS, SLOTS), SLOTS)]
                    for slot, dy, dz in group[tile : tile + 2]
                ]
                side = sides[0] if len(sides) == 1 else jnp.concatenate(sides, axis=1)
                both = jnp.dot(feats, side, preferred_element_type=jnp.float32)
                expo += [both[:, n * SLOTS : (n + 1) * SLOTS] for n in range(len(sides))]
            for slot, dy, dz in group:
                far.append(
                    [
                        jnp.broadcast_to(
                            far_coords[slot, k, cy + dy, pl.ds(cz + dz, 1), :], (8, SLOTS)
                        )
                        for k in range(3)
                    ]
                )
            for chunk in range(SLOTS // 8):
                sel = slice(8 * chunk, 8 * chunk + 8)
                total = [None] * 4 if opening else [acc[cell, chunk, k] for k in range(4)]
                for block, coords in zip(expo, far):
                    w = jnp.exp2(block[sel])
                    terms = [w, w * coords[0], w * coords[1], w * coords[2]]
                    total = [t if old is None else old + t for old, t in zip(total, terms)]
                if closing:
                    column = columns[sel]
                    for k in range(4):
                        summed = jnp.sum(total[k], axis=1, keepdims=True)
                        column = jnp.where(lane8 == cell * 4 + k, summed, column)
                    columns[sel] = column
                else:
                    for k in range(4):
                        acc[cell, chunk, k] = total[k]

    window = [(dy, dz) for dy in range(3) for dz in range(3)]
    phases = [
        [(0, dy, dz) for dy, dz in window[:8]],
        [(0, 2, 2)] + [(1, dy, dz) for dy, dz in window],
        [(2, dy, dz) for dy, dz in window],
    ]

    def sweep(phase):
        @pl.loop(0, CELLS // UNROLL)
        def _(step):
            for part in range(UNROLL):
                pairs(step * UNROLL + part, phases[phase], phase == 0, phase == 2)

    put_mask(0, mask_own[...])

    def turn_body(turn, carry):
        q = qs[turn]
        frame = [q[0:16] - 0.5, q[16:32] + off_y, q[32:48] + off_z]
        put_own(frame)
        put_far(0, q, -0.5)
        sweep(0)

        @pl.when(turn == 0)
        def _():
            for side in range(2):
                mask_copy(side).wait()
            for slot in range(2):
                put_mask(1 + slot, mask_halo[order[slot]])

        for slot in range(2):
            side = order[slot]
            slab_landing(turn, side).wait_recv()
            put_far(1 + slot, halo[turn, side], jnp.where(side == 0, 0.5, -1.5))
            sweep(1 + slot)

        sums[...] = columns[...].T
        for side in range(2):
            slab_copy(turn, side).wait_send()
            bead_copy(turn, side).wait()
        before, behind = chain[turn, 1], chain[turn, 0]
        spring = -SPRING * ((2.0 * q - before) - behind)
        here = jnp.where(mask_own[...] == 0.0, PAIR_SCALE, 0.0)
        total = [sums[pl.ds(k, CELLS, stride=4), :] for k in range(4)]
        finish = jnp.where(turn > 0, HALF_STEP, 0.0)
        begin = jnp.where(turn < STEPS, HALF_STEP, 0.0)
        after = jnp.minimum(turn + 1, STEPS)
        advance = jnp.where(turn < STEPS, TIME_STEP, 0.0)
        for k in range(3):
            sel = slice(16 * k, 16 * k + 16)
            force = (frame[k] * total[0] - total[1 + k]) * here + spring[sel]
            v = vel_out[sel] + finish * force
            v = v + begin * force
            vel_out[sel] = v
            pos_out[sel] = q[sel] + advance * v

        @pl.when(turn < STEPS)
        def _():
            qs[turn + 1] = pos_out[...]
            send(turn + 1)

        return carry

    lax.fori_loop(0, EVALS, turn_body, 0)


def local(positions, velocities, counts):
    rows = 3 * CELLS
    beads, slabs = lax.axis_size("bead"), lax.axis_size("slab")
    f32, bf16 = jnp.float32, jnp.bfloat16
    vmem = pl.BlockSpec(memory_space=pltpu.VMEM)
    out = pl.pallas_call(
        functools.partial(kernel, beads, slabs),
        out_shape=[jax.ShapeDtypeStruct((rows, SLOTS), f32)] * 2,
        in_specs=[vmem, vmem, pl.BlockSpec(memory_space=pltpu.SMEM)],
        out_specs=[vmem, vmem],
        scratch_shapes=[
            pltpu.VMEM((EVALS, rows, SLOTS), f32),
            pltpu.VMEM((EVALS, 2, rows, SLOTS), f32),
            pltpu.VMEM((EVALS, 2, rows, SLOTS), f32),
            pltpu.VMEM((CELLS, SLOTS), f32),
            pltpu.VMEM((2, CELLS, SLOTS), f32),
            pltpu.VMEM((3, 6, 8, SLOTS), f32),
            pltpu.VMEM((CELLS * OWN_STRIDE, SLOTS), f32),
            pltpu.VMEM((3 * 48 * FAR_STRIDE + 8, SLOTS), f32),
            pltpu.VMEM((CELLS, SLOTS, FEATS), bf16),
            pltpu.VMEM((3, 6, FEATS, 6 * SLOTS), bf16),
            pltpu.VMEM((3, 3, 6, 8, SLOTS), f32),
            pltpu.VMEM((CELLS, SLOTS // 8, 4, 8, SLOTS), f32),
            pltpu.VMEM((SLOTS, SLOTS), f32),
            pltpu.VMEM((SLOTS, SLOTS), f32),
            pltpu.VMEM((SLOTS, SLOTS), bf16),
            pltpu.SemaphoreType.DMA((EVALS, 4)),
            pltpu.SemaphoreType.DMA((EVALS, 4)),
            pltpu.SemaphoreType.DMA((2,)),
            pltpu.SemaphoreType.DMA((2,)),
        ],
        compiler_params=pltpu.CompilerParams(collective_id=0, has_side_effects=True),
        name="verlet",
    )(positions.reshape(rows, SLOTS), velocities.reshape(rows, SLOTS), counts)
    return tuple(o.reshape(positions.shape) for o in out)


def solution(mesh):
    spec = P("bead", None, "slab", None, None, None)
    return jax.shard_map(
        local,
        mesh=mesh,
        in_specs=(spec, spec, P("slab", None, None)),
        out_specs=(spec, spec),
        check_vma=False,
    )
```

time: 85.7 us -> 73.2 us (0.85)
  Pallas kernels: 82.8 us -> 70.3 us
    pallas_call x1, Pallas kernels: 82.8 us -> 70.3 us  [local(): pl.pallas_call(functools.partial(kernel, beads, slabs), out_shape=[jax.Sh...]
where the time goes in v1:
time: 73.2 us; the launch traced here: 72.9 us
  Pallas kernels  70.3 us (96%)
  local copies, waits for them, and re-layouts  1.96 us (3%)
    pallas_call x1, Pallas kernels, local(): pl.pallas_call(functools.partial(kernel, beads, slabs), out_shape=[jax.Sh...  70.3 us
    unnamed x4, local copies, waits for them, and re-layouts  1.96 us

profile of v1, /device:TPU:8, one launch (start us, length us, event | category | flops | bytes accessed | tf_op | source)
XLA Modules:
  0.0 72.9 jit_solution(10147625372243138299)
XLA Ops:
  0.6 70.3 %verlet.1 = (f32[48,128]{1,0:T(8,128)}, f32[48,128]{1,0:T(8,128)}) custom-call(f32[48,128]{1,0:T(8,128)} %bitcast.8, f32[48,128]{1,0:T(8,128)} %bitcast.9, s32[1,4,4]{2,1,0:T(4,128)} %counts.1), custom_call_target="tpu_custom_call" | custom-call | tf_op jit(solution)/shard_map/verlet/pallas_call | solution.py:308
  71.0 0.0 copy-start
  71.0 1.4 %copy.9 = f32[1,3,1,4,4,128]{5,4,3,2,1,0:T(4,128)} copy(f32[1,3,1,4,4,128]{5,4,3,2,1,0:T(4,128)} %bitcast.11) | data formatting | bytes 49152
  72.3 0.0 copy-done
  72.3 0.6 copy.10
Async XLA Ops:
  71.0 1.4 %copy-start = (f32[48,128]{1,0:T(8,128)S(1)}, f32[48,128]{1,0:T(8,128)}, u32[]{:S(2)}) copy-start(f32[48,128]{1,0:T(8,128)} %get-tuple-element.5) | copy-start | bytes 73732

commit v2 on v1

--- a/solution.py
+++ b/solution.py
@@ -25,6 +25,7 @@
 FEATS = 32
 OWN_STRIDE, FAR_STRIDE = 33, 25
 UNROLL = 16
+STRIDE = 8
 MESH = pl.DeviceIdType.MESH
 
 
@@ -55,10 +56,10 @@
 
 def kernel(
     beads, slabs,
-    pos_in, vel_in, counts, pos_out, vel_out,
-    qs, halo, chain, mask_own, mask_halo, ext, own32, far32, own_feats, far_feats, far_coords,
+    pos_in, vel_in, counts, out,
+    qs, vel, halo, chain, mask_own, mask_halo, ext, own32, far32, own_feats, far_feats, far_coords,
     acc, columns, sums, eye,
-    send_sem, recv_sem, mask_send, mask_recv,
+    send_sem, recv_sem, mask_send, mask_recv, load_sem,
 ):
     bead, slab = lax.axis_index("bead"), lax.axis_index("slab")
     slab_up, slab_down = lax.rem(slab + 1, slabs), lax.rem(slab + slabs - 1, slabs)
@@ -71,13 +72,16 @@
     for partner in partners:
         pl.semaphore_signal(barrier, inc=1, device_id=partner, device_id_type=MESH)
 
+    load_pos = pltpu.make_async_copy(pos_in, qs.at[0], load_sem.at[0])
+    load_vel = pltpu.make_async_copy(vel_in, vel, load_sem.at[1])
+    load_pos.start()
+    load_vel.start()
+
     lanes = lax.broadcasted_iota(jnp.int32, (1, SLOTS), 1)
     for cell in range(CELLS):
         here = lanes < counts[0, cell // 4, cell % 4]
         mask_own[cell : cell + 1, :] = jnp.where(here, 0.0, ABSENT)
-    qs[0] = pos_in[...]
-    vel_out[...] = vel_in[...]
-
+    load_pos.wait()
     pl.semaphore_wait(barrier, 4)
 
     def mask_copy(side):
@@ -197,9 +201,9 @@
     def pairs(cell, blocks, first, last):
         cy, cz = cell // 4, lax.rem(cell, 4)
         feats = own_feats[cell]
-        for start in range(0, len(blocks), 4):
-            group = blocks[start : start + 4]
-            opening, closing = first and start == 0, last and start + 4 >= len(blocks)
+        for start in range(0, len(blocks), STRIDE):
+            group = blocks[start : start + STRIDE]
+            opening, closing = first and start == 0, last and start + STRIDE >= len(blocks)
             expo, far = [], []
             for tile in range(0, len(group), 2):
                 sides = [
@@ -259,6 +263,7 @@
 
         @pl.when(turn == 0)
         def _():
+            load_vel.wait()
             for side in range(2):
                 mask_copy(side).wait()
             for slot in range(2):
@@ -285,19 +290,20 @@
         for k in range(3):
             sel = slice(16 * k, 16 * k + 16)
             force = (frame[k] * total[0] - total[1 + k]) * here + spring[sel]
-            v = vel_out[sel] + finish * force
+            v = vel[sel] + finish * force
             v = v + begin * force
-            vel_out[sel] = v
-            pos_out[sel] = q[sel] + advance * v
+            vel[sel] = v
+            qs[turn + 1, sel] = q[sel] + advance * v
 
         @pl.when(turn < STEPS)
         def _():
-            qs[turn + 1] = pos_out[...]
             send(turn + 1)
 
         return carry
 
     lax.fori_loop(0, EVALS, turn_body, 0)
+    out[0] = qs[EVALS]
+    out[1] = vel[...]
 
 
 def local(positions, velocities, counts):
@@ -307,11 +313,12 @@
     vmem = pl.BlockSpec(memory_space=pltpu.VMEM)
     out = pl.pallas_call(
         functools.partial(kernel, beads, slabs),
-        out_shape=[jax.ShapeDtypeStruct((rows, SLOTS), f32)] * 2,
-        in_specs=[vmem, vmem, pl.BlockSpec(memory_space=pltpu.SMEM)],
-        out_specs=[vmem, vmem],
+        out_shape=jax.ShapeDtypeStruct((2, rows, SLOTS), f32),
+        in_specs=[pl.BlockSpec(memory_space=pl.ANY)] * 2 + [pl.BlockSpec(memory_space=pltpu.SMEM)],
+        out_specs=vmem,
         scratch_shapes=[
-            pltpu.VMEM((EVALS, rows, SLOTS), f32),
+            pltpu.VMEM((EVALS + 1, rows, SLOTS), f32),
+            pltpu.VMEM((rows, SLOTS), f32),
             pltpu.VMEM((EVALS, 2, rows, SLOTS), f32),
             pltpu.VMEM((EVALS, 2, rows, SLOTS), f32),
             pltpu.VMEM((CELLS, SLOTS), f32),
@@ -330,11 +337,12 @@
             pltpu.SemaphoreType.DMA((EVALS, 4)),
             pltpu.SemaphoreType.DMA((2,)),
             pltpu.SemaphoreType.DMA((2,)),
+            pltpu.SemaphoreType.DMA((2,)),
         ],
         compiler_params=pltpu.CompilerParams(collective_id=0, has_side_effects=True),
         name="verlet",
     )(positions.reshape(rows, SLOTS), velocities.reshape(rows, SLOTS), counts)
-    return tuple(o.reshape(positions.shape) for o in out)
+    return tuple(out[n].reshape(positions.shape) for n in range(2))
 
 
 def solution(mesh):

time: 73.2 us -> 72.3 us (0.988)
    unnamed x4 -> x0, local copies, waits for them, and re-layouts: 1.96 us -> none
    slice x0 -> x1, local copies, waits for them, and re-layouts: none -> 1.38 us  [local(): return tuple((out[n].reshape(positions.shape) for n in range(2)))]
where the time goes in v2:
time: 72.3 us; the launch traced here: 72 us
  Pallas kernels  70 us (97%)
  local copies, waits for them, and re-layouts  1.38 us (2%)
    pallas_call x1, Pallas kernels, local(): pl.pallas_call(functools.partial(kernel, beads, slabs), out_shape=jax.Sha...  70 us

profile of v2, /device:TPU:8, one launch (start us, length us, event | category | flops | bytes accessed | tf_op | source)
XLA Modules:
  0.0 72.0 jit_solution(12746481696638506861)
XLA Ops:
  0.6 70.0 %verlet.1 = f32[2,48,128]{2,1,0:T(8,128)} custom-call(f32[48,128]{1,0:T(8,128)} %bitcast.8, f32[48,128]{1,0:T(8,128)} %bitcast.9, s32[1,4,4]{2,1,0:T(4,128)} %counts.1), custom_call_target="tpu_custom_call" | custom-call | tf_op jit(solution)/shard_map/verlet/pallas_call | solution.py:314
  70.6 1.4 %fusion = (f32[1,48,128]{2,1,0:T(8,128)}, f32[1,48,128]{2,1,0:T(8,128)}) fusion(f32[2,48,128]{2,1,0:T(8,128)} %verlet.1), kind=kLoop, calls=%fused_computation | loop fusion | bytes 98304 | tf_op jit(solution)/shard_map/slice | solution.py:345

commit v3 on v2

--- a/solution.py
+++ b/solution.py
@@ -58,7 +58,7 @@
     beads, slabs,
     pos_in, vel_in, counts, out,
     qs, vel, halo, chain, mask_own, mask_halo, ext, own32, far32, own_feats, far_feats, far_coords,
-    acc, columns, sums, eye,
+    acc, columns, sums,
     send_sem, recv_sem, mask_send, mask_recv, load_sem,
 ):
     bead, slab = lax.axis_index("bead"), lax.axis_index("slab")
@@ -147,10 +147,6 @@
     far32[3 * 48 * FAR_STRIDE :, :] = zero
     ext[...] = jnp.zeros_like(ext)
     columns[...] = jnp.zeros_like(columns)
-    row_id = lax.broadcasted_iota(jnp.int32, (SLOTS, SLOTS), 0)
-    lane_id = lax.broadcasted_iota(jnp.int32, (SLOTS, SLOTS), 1)
-    eye[...] = jnp.where(row_id == lane_id, 1.0, 0.0).astype(jnp.bfloat16)
-
     cell_id = lax.broadcasted_iota(jnp.int32, (CELLS, SLOTS), 0)
     off_y = (cell_id // 4).astype(jnp.float32) - 2.0
     off_z = (cell_id % 4).astype(jnp.float32) - 2.0
@@ -192,11 +188,8 @@
             for k, row in own_rows([coord[sel] for coord in coords]):
                 own32[pl.ds(8 * half * OWN_STRIDE + k, 8, stride=OWN_STRIDE), :] = row
         for cell in range(CELLS):
-            block = own32[cell * OWN_STRIDE : cell * OWN_STRIDE + FEATS, :].astype(jnp.bfloat16)
-            turned = lax.dot_general(
-                eye[...], block, (((1,), (1,)), ((), ())), preferred_element_type=jnp.float32
-            )
-            own_feats[cell] = turned.astype(jnp.bfloat16)
+            block = own32[cell * OWN_STRIDE : cell * OWN_STRIDE + FEATS, :]
+            own_feats[cell] = block.T.astype(jnp.bfloat16)
 
     def pairs(cell, blocks, first, last):
         cy, cz = cell // 4, lax.rem(cell, 4)
@@ -332,7 +325,6 @@
             pltpu.VMEM((CELLS, SLOTS // 8, 4, 8, SLOTS), f32),
             pltpu.VMEM((SLOTS, SLOTS), f32),
             pltpu.VMEM((SLOTS, SLOTS), f32),
-            pltpu.VMEM((SLOTS, SLOTS), bf16),
             pltpu.SemaphoreType.DMA((EVALS, 4)),
             pltpu.SemaphoreType.DMA((EVALS, 4)),
             pltpu.SemaphoreType.DMA((2,)),

time: 72.3 us -> 71.6 us (level)
  no operation moved by 1% of the time
where the time goes in v3:
time: 71.6 us; the launch traced here: 71.4 us
  Pallas kernels  69.3 us (97%)
  local copies, waits for them, and re-layouts  1.38 us (2%)
    pallas_call x1, Pallas kernels, local(): pl.pallas_call(functools.partial(kernel, beads, slabs), out_shape=jax.Sha...  69.3 us

profile of v3, /device:TPU:8, one launch (start us, length us, event | category | flops | bytes accessed | tf_op | source)
XLA Modules:
  0.0 71.4 jit_solution(682679247460319778)
XLA Ops:
  0.6 69.3 %verlet.1 = f32[2,48,128]{2,1,0:T(8,128)} custom-call(f32[48,128]{1,0:T(8,128)} %bitcast.8, f32[48,128]{1,0:T(8,128)} %bitcast.9, s32[1,4,4]{2,1,0:T(4,128)} %counts.1), custom_call_target="tpu_custom_call" | custom-call | tf_op jit(solution)/shard_map/verlet/pallas_call | solution.py:307
  70.0 1.4 %fusion = (f32[1,48,128]{2,1,0:T(8,128)}, f32[1,48,128]{2,1,0:T(8,128)}) fusion(f32[2,48,128]{2,1,0:T(8,128)} %verlet.1), kind=kLoop, calls=%fused_computation | loop fusion | bytes 98304 | tf_op jit(solution)/shard_map/slice | solution.py:337
